TPU v7x, 32 devices: a whole 2x2x4 slice. The times are simulated.
32 devices in a mesh: shard: 4 (over z), ctx: 4 (over x, core), tp: 2 (over y).
Axes of the slice: x: 2, y: 2, z: 4, core: 2. Of those that a mesh axis runs over, the one named last changes fastest.
Arguments:
- hidden_in: bfloat16 [4, 1024, 1024], P('shard', 'ctx'), may hold values from -6 to 6
- out_grad: bfloat16 [4, 1024, 1024], P('shard', 'ctx'), may hold values from -6 to 6
- segment_ids: int32 [4, 1024], P('shard'), may hold values from 0 to 3, never falling along the last dimension, each value on 1 to 512 neighbouring positions
- w_qkv: bfloat16 [3, 1024, 1024], P(None, 'shard', 'tp'), may hold values from -0.1875 to 0.1875
- bias_qv: float32 [2, 1024], P(None, 'tp'), may hold values from -3 to 3
- w_out: bfloat16 [1024, 1024], P('tp', 'shard'), may hold values from -0.75 to 0.75
- bias_out: float32 [1024], replicated, may hold values from -3 to 3
- norm1_gain: float32 [1024], replicated, may hold values from 0.5 to 1.5
- norm1_shift: float32 [1024], replicated, may hold values from -3 to 3
- w_up: bfloat16 [1024, 4096], P('shard', 'tp'), may hold values from -0.1875 to 0.1875
- bias_up: float32 [4096], P('tp'), may hold values from -3 to 3
- w_down: bfloat16 [4096, 1024], P('tp', 'shard'), may hold values from -0.09375 to 0.09375
- bias_down: float32 [1024], replicated, may hold values from -3 to 3
- norm2_gain: float32 [1024], replicated, may hold values from 0.5 to 1.5
- norm2_shift: float32 [1024], replicated, may hold values from -3 to 3
Outputs:
- output: bfloat16 [4, 1024, 1024], P('shard', 'ctx')
- input_grad: bfloat16 [4, 1024, 1024], P('shard', 'ctx')
- w_qkv_grad: float32 [3, 1024, 1024], P(None, 'shard', 'tp')
- bias_qv_grad: float32 [2, 1024], P(None, 'tp')
- w_out_grad: float32 [1024, 1024], P('tp', 'shard')
- bias_out_grad: float32 [1024], replicated
- norm1_gain_grad: float32 [1024], replicated
- norm1_shift_grad: float32 [1024], replicated
- w_up_grad: float32 [1024, 4096], P('shard', 'tp')
- bias_up_grad: float32 [4096], P('tp')
- w_down_grad: float32 [4096, 1024], P('tp', 'shard')
- bias_down_grad: float32 [1024], replicated
- norm2_gain_grad: float32 [1024], replicated
- norm2_shift_grad: float32 [1024], replicated
Inputs may be any that keep to these rules, and one draw needn't show every extreme that they name: `segment_ids`: within each sequence the ids never fall and start at 0; each document has at most 512 tokens, and some document has exactly that many.
All inputs are finite; a program needn't handle non-finite values.
Results may differ from a plain program's by a relative error of at most 0.022.
The roundings to bfloat16 on the way count: a program that leaves them out, or rounds other values in their place, can miss the bound.
Values may be sent and summed in bfloat16 or wider, within the bound.
A program may use at most 128 MiB of HBM per device.

v0:
```python
import math
import jax
import jax.numpy as jnp
from jax import lax
from jax.sharding import PartitionSpec as P

HEADS = 16
EPSILON = 1e-05


def normalize(resid, gain, shift):
    average = jnp.mean(resid, axis=-1, keepdims=True)
    centred = resid - average
    variance = jnp.mean(centred * centred, axis=-1, keepdims=True)
    inv_std = lax.rsqrt(variance + EPSILON)
    normed = centred * inv_std
    return (normed * gain + shift, normed, inv_std)


def normalize_back(cotan, normed, inv_std, gain):
    scaled = cotan * gain
    return inv_std * (
        scaled
        - jnp.mean(scaled, axis=-1, keepdims=True)
        - normed * jnp.mean(scaled * normed, axis=-1, keepdims=True)
    )


def gelu_value(pre_act):
    return 0.5 * pre_act * (1.0 + jax.scipy.special.erf(pre_act * 0.7071067811865476))


def gelu_slope(pre_act):
    return (
        0.5 * (1.0 + jax.scipy.special.erf(pre_act * 0.7071067811865476))
        + pre_act * jnp.exp(-0.5 * pre_act * pre_act) * 0.3989422804014327
    )


def block_scores(query_block, keys, ids_block, ids_whole, scale):
    scores = (
        jnp.einsum("qhe,khe->hqk", query_block, keys, preferred_element_type=jnp.float32) * scale
    )
    return jnp.where((ids_block[:, None] == ids_whole[None, :])[None], scores, -jnp.inf)


def shards(
    hidden_in,
    out_grad,
    segment_ids,
    w_qkv,
    bias_qv,
    w_out,
    bias_out,
    norm1_gain,
    norm1_shift,
    w_up,
    bias_up,
    w_down,
    bias_down,
    norm2_gain,
    norm2_shift,
):
    seq_count, local_len, width = hidden_in.shape
    ctx_count = lax.axis_size("ctx")
    full_len = local_len * ctx_count
    row_count = seq_count * local_len
    head_dim = width // HEADS
    scale = 1.0 / math.sqrt(head_dim)
    qkv_full, out_full, up_full, down_full = (
        lax.all_gather(w_qkv, "shard", axis=1, tiled=True),
        lax.all_gather(w_out, "shard", axis=1, tiled=True),
        lax.all_gather(w_up, "shard", axis=0, tiled=True),
        lax.all_gather(w_down, "shard", axis=1, tiled=True),
    )
    local_cols = qkv_full.shape[2]
    group_cols = local_cols // ctx_count
    local_heads = group_cols // head_dim
    block_rows = min(512, full_len)
    block_count = full_len // block_rows
    tokens = hidden_in.reshape(row_count, width)
    bias_three = jnp.stack([bias_qv[0], jnp.zeros_like(bias_qv[0]), bias_qv[1]])
    project = (
        jnp.einsum("td,kde->tke", tokens, qkv_full, preferred_element_type=jnp.float32)
        + bias_three[None]
    )
    project = project.astype(jnp.bfloat16).reshape(seq_count, local_len, 3, ctx_count, group_cols)
    heads = lax.all_to_all(project, "ctx", split_axis=3, concat_axis=1, tiled=True)
    heads = heads.reshape(seq_count, full_len, 3, local_heads, head_dim)

    def attend_sequence(packed):
        seq_heads, seq_ids = packed
        keys = seq_heads[:, 1]
        values = seq_heads[:, 2]
        queries = seq_heads[:, 0].reshape(block_count, block_rows, local_heads, head_dim)
        id_blocks = seq_ids.reshape(block_count, block_rows)

        def attend_block(piece):
            query_block, ids_block = piece
            scores = block_scores(query_block, keys, ids_block, seq_ids, scale)
            log_total = jax.nn.logsumexp(scores, axis=-1)
            probs_low = jnp.exp(scores - log_total[..., None]).astype(jnp.bfloat16)
            attended = jnp.einsum(
                "hqk,khe->qhe", probs_low, values, preferred_element_type=jnp.float32
            ).astype(jnp.bfloat16)
            return (attended, log_total)

        attended, log_total = lax.map(attend_block, (queries, id_blocks))
        return (attended.reshape(full_len, local_heads, head_dim), log_total)

    attended_heads, log_totals = lax.map(attend_sequence, (heads, segment_ids))
    attended_tok = lax.all_to_all(
        attended_heads.reshape(seq_count, full_len, 1, group_cols),
        "ctx",
        split_axis=1,
        concat_axis=2,
        tiled=True,
    )
    attended_tok = attended_tok.reshape(row_count, local_cols)
    attn_part = jnp.dot(attended_tok, out_full, preferred_element_type=jnp.float32)
    resid_one = (
        lax.psum(attn_part.astype(jnp.bfloat16), "tp").astype(jnp.float32)
        + bias_out
        + tokens.astype(jnp.float32)
    )
    first, normed_one, inv_one = normalize(resid_one, norm1_gain, norm1_shift)
    first_low = first.astype(jnp.bfloat16)
    pre_act = jnp.dot(first_low, up_full, preferred_element_type=jnp.float32) + bias_up
    activated = gelu_value(pre_act).astype(jnp.bfloat16)
    ffn_part = jnp.dot(activated, down_full, preferred_element_type=jnp.float32)
    resid_two = (
        lax.psum(ffn_part.astype(jnp.bfloat16), "tp").astype(jnp.float32) + bias_down + first
    )
    result, normed_two, inv_two = normalize(resid_two, norm2_gain, norm2_shift)
    grad_float = out_grad.reshape(row_count, width).astype(jnp.float32)
    gain_two_grad = jnp.sum(grad_float * normed_two, axis=0)
    shift_two_grad = jnp.sum(grad_float, axis=0)
    resid_two_grad = normalize_back(grad_float, normed_two, inv_two, norm2_gain)
    resid_two_low = resid_two_grad.astype(jnp.bfloat16)
    bias_down_grad = jnp.sum(resid_two_grad, axis=0)
    act_grad = jnp.dot(resid_two_low, down_full.T, preferred_element_type=jnp.float32)
    pre_grad = act_grad * gelu_slope(pre_act)
    pre_low = pre_grad.astype(jnp.bfloat16)
    bias_up_grad = jnp.sum(pre_grad, axis=0)
    back_part = jnp.dot(pre_low, up_full.T, preferred_element_type=jnp.float32)
    first_grad = resid_two_grad + lax.psum(back_part.astype(jnp.bfloat16), "tp").astype(jnp.float32)
    gain_one_grad = jnp.sum(first_grad * normed_one, axis=0)
    shift_one_grad = jnp.sum(first_grad, axis=0)
    resid_one_grad = normalize_back(first_grad, normed_one, inv_one, norm1_gain)
    resid_one_low = resid_one_grad.astype(jnp.bfloat16)
    bias_out_grad = jnp.sum(resid_one_grad, axis=0)
    attended_grad = jnp.dot(resid_one_low, out_full.T, preferred_element_type=jnp.float32).astype(
        jnp.bfloat16
    )
    grad_heads = lax.all_to_all(
        attended_grad.reshape(seq_count, local_len, ctx_count, group_cols),
        "ctx",
        split_axis=2,
        concat_axis=1,
        tiled=True,
    )
    grad_heads = grad_heads.reshape(seq_count, full_len, local_heads, head_dim)

    def back_sequence(packed):
        seq_heads, seq_ids, seq_attended, seq_grad, seq_log = packed
        keys = seq_heads[:, 1]
        values = seq_heads[:, 2]
        queries = seq_heads[:, 0].reshape(block_count, block_rows, local_heads, head_dim)
        id_blocks = seq_ids.reshape(block_count, block_rows)
        att_blocks = seq_attended.reshape(block_count, block_rows, local_heads, head_dim)
        grad_blocks = seq_grad.reshape(block_count, block_rows, local_heads, head_dim)

        def back_block(carry, piece):
            key_total, value_total = carry
            query_block, ids_block, att_block, grad_block, log_block = piece
            scores = block_scores(query_block, keys, ids_block, seq_ids, scale)
            probs = jnp.exp(scores - log_block[..., None])
            probs_low = probs.astype(jnp.bfloat16)
            prob_grad = jnp.einsum(
                "qhe,khe->hqk", grad_block, values, preferred_element_type=jnp.float32
            )
            offset = jnp.sum(
                grad_block.astype(jnp.float32) * att_block.astype(jnp.float32), axis=-1
            ).T
            score_grad = (probs * (prob_grad - offset[..., None]) * scale).astype(jnp.bfloat16)
            query_grad = jnp.einsum(
                "hqk,khe->qhe", score_grad, keys, preferred_element_type=jnp.float32
            ).astype(jnp.bfloat16)
            key_total = key_total + jnp.einsum(
                "hqk,qhe->khe", score_grad, query_block, preferred_element_type=jnp.float32
            )
            value_total = value_total + jnp.einsum(
                "hqk,qhe->khe", probs_low, grad_block, preferred_element_type=jnp.float32
            )
            return ((key_total, value_total), query_grad)

        empty = jnp.zeros((full_len, local_heads, head_dim), jnp.float32)
        (key_total, value_total), query_grads = lax.scan(
            back_block, (empty, empty), (queries, id_blocks, att_blocks, grad_blocks, seq_log)
        )
        return jnp.stack(
            [
                query_grads.reshape(full_len, local_heads, head_dim),
                key_total.astype(jnp.bfloat16),
                value_total.astype(jnp.bfloat16),
            ],
            axis=1,
        )

    head_grads = lax.map(
        back_sequence, (heads, segment_ids, attended_heads, grad_heads, log_totals)
    )
    proj_grad = lax.all_to_all(
        head_grads.reshape(seq_count, full_len, 3, 1, group_cols),
        "ctx",
        split_axis=1,
        concat_axis=3,
        tiled=True,
    )
    proj_grad = proj_grad.reshape(row_count, 3, local_cols)
    bias_qv_grad = jnp.stack(
        [
            jnp.sum(proj_grad[:, 0].astype(jnp.float32), axis=0),
            jnp.sum(proj_grad[:, 2].astype(jnp.float32), axis=0),
        ]
    )
    input_part = jnp.einsum("tke,kde->td", proj_grad, qkv_full, preferred_element_type=jnp.float32)
    input_grad = (
        resid_one_grad + lax.psum(input_part.astype(jnp.bfloat16), "tp").astype(jnp.float32)
    ).astype(jnp.bfloat16)
    shard_rows = width // lax.axis_size("shard")
    part_qkv = jnp.einsum(
        "td,tke->dke", tokens, proj_grad, preferred_element_type=jnp.float32
    ).reshape(shard_rows * lax.axis_size("shard"), 3 * local_cols)
    part_out = jnp.einsum(
        "td,te->de", resid_one_low, attended_tok, preferred_element_type=jnp.float32
    )
    part_up = jnp.einsum("td,te->de", first_low, pre_low, preferred_element_type=jnp.float32)
    part_down = jnp.einsum(
        "td,te->de", resid_two_low, activated, preferred_element_type=jnp.float32
    )
    owned = lax.psum_scatter(
        jnp.concatenate([part_qkv, part_out, part_up, part_down], axis=1).astype(jnp.bfloat16),
        "shard",
        scatter_dimension=0,
        tiled=True,
    ).astype(jnp.float32)
    owned = lax.psum(owned.astype(jnp.bfloat16), "ctx").astype(jnp.float32)
    owned_rows = owned.shape[0]
    hidden_cols = pre_low.shape[1]
    qkv_grad = owned[:, : 3 * local_cols].reshape(owned_rows, 3, local_cols).transpose(1, 0, 2)
    out_weight_grad = owned[:, 3 * local_cols : 4 * local_cols].T
    up_grad = owned[:, 4 * local_cols : 4 * local_cols + hidden_cols]
    down_grad = owned[:, 4 * local_cols + hidden_cols :].T
    small = lax.psum(
        (
            bias_qv_grad,
            bias_out_grad,
            gain_one_grad,
            shift_one_grad,
            bias_up_grad,
            bias_down_grad,
            gain_two_grad,
            shift_two_grad,
        ),
        ("shard", "ctx"),
    )
    output = result.astype(jnp.bfloat16).reshape(seq_count, local_len, width)
    return (
        output,
        input_grad.reshape(seq_count, local_len, width),
        qkv_grad,
        small[0],
        out_weight_grad,
        small[1],
        small[2],
        small[3],
        up_grad,
        small[4],
        down_grad,
        small[5],
        small[6],
        small[7],
    )


def solution(mesh):
    return jax.shard_map(
        shards,
        mesh=mesh,
        in_specs=(
            P("shard", "ctx", None),
            P("shard", "ctx", None),
            P("shard", None),
            P(None, "shard", "tp"),
            P(None, "tp"),
            P("tp", "shard"),
            P(),
            P(),
            P(),
            P("shard", "tp"),
            P("tp"),
            P("tp", "shard"),
            P(),
            P(),
            P(),
        ),
        out_specs=(
            P("shard", "ctx", None),
            P("shard", "ctx", None),
            P(None, "shard", "tp"),
            P(None, "tp"),
            P("tp", "shard"),
            P(),
            P(),
            P(),
            P("shard", "tp"),
            P("tp"),
            P("tp", "shard"),
            P(),
            P(),
            P(),
        ),
        check_vma=False,
    )
```

profile of v0, /device:TPU:0, one launch (start us, length us, event | category | flops | bytes accessed | tf_op | source)
XLA Modules:
  0.0 789.5 jit_solution(12445965865894515886)
XLA Ops:
  8.8 66.9 %all-gather.5.cloned.1.call-done = bf16[3,1024,512]{2,1,0:T(8,128)(2,1)} async-done(((bf16[3,256,512]{2,1,0:T(8,128)(2,1)}), bf16[3,1024,512]{2,1,0:T(8,128)(2,1)}) %all-gather.5.cloned.1.call-update) | async-done | bytes 3145744 | tf_op jit(solution)/shard_map/all_gather | solution.py:71
  75.8 3.0 add_convert_fusion
  80.0 3.5 all-to-all-start
  85.5 9.6 %all-to-all-done = bf16[1,256,3,4,128]{4,1,2,0,3:T(8,128)(2,1)S(1)} async-done(((bf16[1,256,3,4,128]{4,1,2,0,3:T(8,128)(2,1)}), bf16[1,256,3,4,128]{4,1,2,0,3:T(8,128)(2,1)S(1)}, u32[]{:S(2)}, u32[]{:S(2)}) %all-to-all-start) | async-done | bytes 786464 | tf_op jit(solution)/shard_map/all_to_all | solution.py:88
  96.7 7.9 %while.45 = (s32[]{:T(128)}, bf16[2,512,2,64]{1,3,2,0:T(8,128)(2,1)S(1)}, f32[2,2,512]{2,1,0:T(2,128)S(1)}, s32[2,512]{1,0:T(2,128)S(1)}, s32[1024]{0:T(1024)S(1...) while((s32[]{:T(128)}, ...), condition=%wide.region_3.4_spmd, body=%wide.region_0.3_spmd.sunk | while | flops 280567808 | bytes 15526005 | solution.py:108
  105.9 2.3 reduce.7
  108.2 8.4 %all_to_all.60 = bf16[4,2,16384]{2,1,0:T(2,128)(2,1)S(1)} all-to-all(bf16[4,2,16384]{2,1,0:T(2,128)(2,1)S(1)} %reshape.279), channel_id=1, replica_groups=mesh['shard'=4,'ctx'=4,'tp'=2] {'ctx'}, dimensions={0} | all-to-all | bytes 524288 | tf_op jit(solution)/shard_map/all_to_all | solution.py:112
  117.2 2.6 convolution_convert_fusion.5
  121.1 25.2 %all-reduce.7.cloned.1.call-done = bf16[256,1024]{1,0:T(8,128)(2,1)} async-done(((bf16[256,1024]{1,0:T(8,128)(2,1)}), bf16[256,1024]{1,0:T(8,128)(2,1)}) %all-reduce.7.cloned.1.call-update) | async-done | bytes 524304 | tf_op jit(solution)/shard_map/psum | solution.py:122
  147.6 1.4 multiply_reduce_fusion.3
  149.0 79.5 %all-gather.9.cloned.1.call-done = bf16[1024,2048]{1,0:T(8,128)(2,1)} async-done(((bf16[256,2048]{1,0:T(8,128)(2,1)}), bf16[1024,2048]{1,0:T(8,128)(2,1)}) %all-gather.9.cloned.1.call-update) | async-done | bytes 4194320 | tf_op jit(solution)/shard_map/all_gather | solution.py:73
  228.5 5.6 multiply_convert_fusion.1
  234.1 74.8 %all-gather.11.cloned.1.call-done = bf16[2048,1024]{1,0:T(8,128)(2,1)} async-done(((bf16[2048,256]{1,0:T(8,128)(2,1)}), bf16[2048,1024]{1,0:T(8,128)(2,1)}) %all-gather.11.cloned.1.call-update) | async-done | bytes 4194320 | tf_op jit(solution)/shard_map/all_gather | solution.py:74
  309.0 4.6 convolution_convert_fusion.7
  313.6 26.9 %all-reduce.9.cloned.1.call-done = bf16[256,1024]{1,0:T(8,128)(2,1)} async-done(((bf16[256,1024]{1,0:T(8,128)(2,1)}), bf16[256,1024]{1,0:T(8,128)(2,1)}) %all-reduce.9.cloned.1.call-update) | async-done | bytes 524304 | tf_op jit(solution)/shard_map/psum | solution.py:132
  340.6 1.7 fusion.74
  344.4 2.1 fusion.76
  347.5 2.1 convolution_convert_fusion.6
  349.7 28.8 %all-reduce.11.cloned.1.call-done = bf16[256,1024]{1,0:T(8,128)(2,1)} async-done(((bf16[256,1024]{1,0:T(8,128)(2,1)}), bf16[256,1024]{1,0:T(8,128)(2,1)}) %all-reduce.11.cloned.1.call-update) | async-done | bytes 524304 | tf_op jit(solution)/shard_map/psum | solution.py:146
  378.5 1.9 multiply_reduce_fusion
  380.4 1.5 fusion.73
  384.1 1.8 copy.118
  385.9 4.3 all-to-all-start.2
  390.1 4.6 convolution_convert_fusion.2
  397.4 12.0 %while.46 = (s32[]{:T(128)}, f32[1024,2,64]{0,2,1:T(8,128)S(1)}, f32[1024,2,64]{0,2,1:T(8,128)}, bf16[2,512,2,64]{1,3,2,0:T(8,128)(2,1)S(1)}, bf16[2,512,2,64]{1...) while((s32[]{:T(128)}, f32[1024,2,64]{0,2,1:T(8,128)S(1)}, ...), condition=%wide.region_17.18_spmd.clone, body=%wide.region_15.17_spmd.clone.sunk | while | flops 683998208 | bytes 29526284 | solution.py:198
  398.6 1.4 fusion.140
  400.0 2.0 multiply_convert_fusion.3
  404.6 1.4 fusion.140
  406.0 2.0 multiply_convert_fusion.3
  411.0 1.4 copy.106
  412.4 4.2 all-to-all-start.3
  416.8 4.5 convolution_convert_fusion.1
  423.1 8.1 %all-to-all-done.3 = bf16[1,1024,3,1,128]{4,2,3,0,1:T(4,128)(2,1)} async-done(((bf16[1,1024,3,1,128]{4,2,3,0,1:T(4,128)(2,1)}), bf16[1,1024,3,1,128]{4,2,3,0,1:T(4,128)(2,1)}, u32[]{:S(2)}, u32[]{:S(2)}) %all-to-all-start.3) | async-done | bytes 786464 | tf_op jit(solution)/shard_map/all_to_all | solution.py:213
  432.5 1.5 copy.108
  434.0 1.6 reshape.260
  435.7 2.7 convolution_convert_fusion.3
  438.4 4.6 copy.110
  443.0 10.9 %pad_maximum_fusion = bf16[1024,6144]{1,0:T(8,128)(2,1)} fusion(bf16[1024,2048]{1,0:T(8,128)(2,1)} %convolution_convert_fusion.1, bf16[1024,2048]{1,0:T(8,128)(2,1)} %convolution_convert_fusion.2, bf16[1024,512]{1,0:T(8,128)(2,1)} %copy.111, bf16[1024,1536]{1,0:T(8,128)(2,1)} %copy.110), kind=kLoop, calls=%fused_computation.55 | loop fusion | flops 50331648 | bytes 25165824 | tf_op jit(solution)/shard_map/concatenate | solution.py:243
  454.2 3.7 fusion.53
  458.0 207.0 %reduce-scatter.2.cloned.1.call-done = bf16[256,6144]{1,0:T(8,128)(2,1)} async-done(((bf16[1024,6144]{1,0:T(8,128)(2,1)}), bf16[256,6144]{1,0:T(8,128)(2,1)}) %reduce-scatter.2.cloned.1.call-update) | async-done | bytes 3145744 | tf_op jit(solution)/shard_map/reduce_scatter | solution.py:242
  665.3 62.3 %all-reduce = (f32[2,512]{1,0:T(2,128)}, f32[1024]{0:T(1024)}, f32[1024]{0:T(1024)}, f32[1024]{0:T(1024)}, f32[2048]{0:T(1024)}, /*index=5*/f32[1024]{0:T(1024)}, f32[1024]{0:T(1024)}, f32[1024]{0:T(1024)}) all-reduce(f32[2,512]{1,0:T(2,128)S(1)} %pad_maximum_fusion.3, ...), channel_id=1, replica_groups=mesh['shard'=4,'ctx'=4,'tp'=2] {'shard','ctx'}, use_global_device_ids=true, to_apply=%region_23.24 | all-reduce | flops 9216 | bytes 73728 | tf_op jit(solution)/shard_map/psum | solution.py:255
  727.6 2.0 fusion.61
  729.6 39.1 %all-reduce.15.cloned.1.call-done = bf16[256,6144]{1,0:T(8,128)(2,1)} async-done(((bf16[256,6144]{1,0:T(8,128)(2,1)}), bf16[256,6144]{1,0:T(8,128)(2,1)}) %all-reduce.15.cloned.1.call-update) | async-done | bytes 3145744 | tf_op jit(solution)/shard_map/psum | solution.py:248
  768.7 2.6 convert_element_type.134
  772.2 1.5 slice_bitcast_fusion
  774.4 1.6 copy.113
  776.0 2.9 copy.115
  779.9 2.8 slice.60
  (168 shorter events, 39.4 us)
Async XLA Ops:
  7.2 68.6 %all-gather.5.cloned.1.call-start = ((), (), s32[]{:S(2)}) async-start(), calls=%async_computation.5 | async-start | bytes 3932160 | tf_op jit(solution)/shard_map/all_gather | solution.py:71
  8.8 76.0 %copy-start.14 = (s32[1,1024]{1,0:T(1,128)S(1)}, s32[1,1024]{1,0:T(1,128)}, u32[]{:S(2)}) copy-start(s32[1,1024]{1,0:T(1,128)} %param.21) | copy-start | bytes 12292
  80.0 15.1 %all-to-all-start = ((bf16[1,256,3,4,128]{4,1,2,0,3:T(8,128)(2,1)}), bf16[1,256,3,4,128]{4,1,2,0,3:T(8,128)(2,1)S(1)}, u32[]{:S(2)}, u32[]{:S(2)}) async-start(bf16[1,256,3,4,128]{4,1,2,0,3:T(8,128)(2,1)} %copy.95), calls=%async_computation | async-start | bytes 1572864 | tf_op jit(solution)/shard_map/all_to_all | solution.py:88
  83.5 33.6 %all-gather.7.cloned.1.call-start = ((), (), s32[]{:S(2)}) async-start(), calls=%async_computation.6 | async-start | bytes 1310720 | tf_op jit(solution)/shard_map/all_gather | solution.py:72
  84.3 62.0 %all-reduce.7.cloned.1.call-start = ((), (), s32[]{:S(2)}) async-start(), calls=%async_computation.7 | async-start | bytes 1048576 | tf_op jit(solution)/shard_map/psum | solution.py:122
  104.6 0.8 copy-start.16
  105.9 40.4 %copy-start = (bf16[1,256,1024]{2,1,0:T(8,128)(2,1)S(1)}, bf16[1,256,1024]{2,1,0:T(8,128)(2,1)}, u32[]{:S(2)}) copy-start(bf16[1,256,1024]{2,1,0:T(8,128)(2,1)} %param.19) | copy-start | bytes 1572868
  105.9 40.4 %copy-start.15 = (f32[1024]{0:T(1024)S(1)}, f32[1024]{0:T(1024)}, u32[]{:S(2)}) copy-start(f32[1024]{0:T(1024)} %param.25) | copy-start | bytes 12292
  116.6 111.9 %copy-start.18 = (f32[1024]{0:T(1024)S(1)}, f32[1024]{0:T(1024)}, u32[]{:S(2)}) copy-start(f32[1024]{0:T(1024)} %param.26) | copy-start | bytes 12292
  116.6 111.9 %copy-start.19 = (f32[1024]{0:T(1024)S(1)}, f32[1024]{0:T(1024)}, u32[]{:S(2)}) copy-start(f32[1024]{0:T(1024)} %param.27) | copy-start | bytes 12292
  116.6 111.9 %copy-start.25 = (f32[2048]{0:T(1024)S(1)}, f32[2048]{0:T(1024)}, u32[]{:S(2)}) copy-start(f32[2048]{0:T(1024)} %param.29) | copy-start | bytes 24580
  117.1 117.0 %copy-start.8 = (bf16[1,256,4,1,128]{1,4,2,3,0:T(8,128)(2,1)}, bf16[1,256,4,1,128]{1,4,2,3,0:T(8,128)(2,1)S(1)}, u32[]{:S(2)}) copy-start(bf16[1,256,4,1,128]{1,4,2,3,0:T(8,128)(2,1)S(1)} %copy.100) | copy-start | bytes 786436
  119.7 108.7 %all-gather.9.cloned.1.call-start = ((), (), s32[]{:S(2)}) async-start(), calls=%async_computation.8 | async-start | bytes 5242880 | tf_op jit(solution)/shard_map/all_gather | solution.py:73
  120.3 188.6 %all-gather.11.cloned.1.call-start = ((), (), s32[]{:S(2)}) async-start(), calls=%async_computation.9 | async-start | bytes 5242880 | tf_op jit(solution)/shard_map/all_gather | solution.py:74
  120.9 219.7 %all-reduce.9.cloned.1.call-start = ((), (), s32[]{:S(2)}) async-start(), calls=%async_computation.10 | async-start | bytes 1048576 | tf_op jit(solution)/shard_map/psum | solution.py:132
  234.1 106.5 %copy-start.1 = (bf16[256,1024]{1,0:T(8,128)(2,1)S(1)}, bf16[256,1024]{1,0:T(8,128)(2,1)}, u32[]{:S(2)}) copy-start(bf16[256,1024]{1,0:T(8,128)(2,1)} %all-reduce.7.cloned.1.call-done) | copy-start | bytes 1572868
  234.1 106.5 %copy-start.21 = (f32[1024]{0:T(1024)S(1)}, f32[1024]{0:T(1024)}, u32[]{:S(2)}) copy-start(f32[1024]{0:T(1024)} %param.31) | copy-start | bytes 12292
  309.0 33.6 %copy-start.5 = (bf16[1,256,1024]{2,1,0:T(8,128)(2,1)S(1)}, bf16[1,256,1024]{2,1,0:T(8,128)(2,1)}, u32[]{:S(2)}) copy-start(bf16[1,256,1024]{2,1,0:T(8,128)(2,1)} %param.20) | copy-start | bytes 1572868
  309.0 33.7 %copy-start.20 = (f32[1024]{0:T(1024)S(1)}, f32[1024]{0:T(1024)}, u32[]{:S(2)}) copy-start(f32[1024]{0:T(1024)} %param.32) | copy-start | bytes 12292
  313.6 29.6 %copy-start.22 = (f32[1024]{0:T(1024)S(1)}, f32[1024]{0:T(1024)}, u32[]{:S(2)}) copy-start(f32[1024]{0:T(1024)} %param.33) | copy-start | bytes 12292
  313.6 64.9 %all-reduce.11.cloned.1.call-start = ((), (), s32[]{:S(2)}) async-start(), calls=%async_computation.11 | async-start | bytes 1048576 | tf_op jit(solution)/shard_map/psum | solution.py:146
  340.6 3.8 copy-start.24
  340.6 3.8 copy-start.26
  344.4 3.1 copy-start.23
  346.6 1.0 copy-start.11
  378.5 4.4 copy-start.7
  381.9 1.0 copy-start.2
  385.9 10.1 %all-to-all-start.2 = ((bf16[1,256,4,128]{1,3,0,2:T(8,128)(2,1)}), bf16[1,256,4,128]{1,3,0,2:T(8,128)(2,1)}, u32[]{:S(2)}, u32[]{:S(2)}) async-start(bf16[1,256,4,128]{1,3,0,2:T(8,128)(2,1)} %bitcast.233), calls=%async_computation.2 | async-start | bytes 524288 | tf_op jit(solution)/shard_map/all_to_all | solution.py:155
  397.4 1.2 copy-start.12
  398.6 1.4 copy-start.17
  400.0 2.0 copy-start.13
  403.4 1.2 copy-start.12
  404.6 1.4 copy-start.17
  406.0 2.0 copy-start.13
  412.4 18.7 %all-to-all-start.3 = ((bf16[1,1024,3,1,128]{4,2,3,0,1:T(4,128)(2,1)}), bf16[1,1024,3,1,128]{4,2,3,0,1:T(4,128)(2,1)}, u32[]{:S(2)}, u32[]{:S(2)}) async-start(bf16[1,1024,3,1,128]{4,2,3,0,1:T(4,128)(2,1)} %copy.106), calls=%async_computation.3 | async-start | bytes 2097152 | tf_op jit(solution)/shard_map/all_to_all | solution.py:213
  416.7 4.6 copy-start.3
  416.7 4.6 copy-start.9
  416.7 248.3 %reduce-scatter.2.cloned.1.call-start = ((), (), s32[]{:S(2)}) async-start(), calls=%async_computation.13 | async-start | bytes 15728640 | tf_op jit(solution)/shard_map/reduce_scatter | solution.py:242
  453.9 211.2 %copy-start.6 = (bf16[1,256,1024]{2,1,0:T(8,128)(2,1)S(1)}, bf16[1,256,1024]{2,1,0:T(8,128)(2,1)}, u32[]{:S(2)}) copy-start(bf16[1,256,1024]{2,1,0:T(8,128)(2,1)} %param.20) | copy-start | bytes 1572868
  453.9 273.7 %all-reduce.13.cloned.1.call-start = ((), (), s32[]{:S(2)}) async-start(), calls=%async_computation.12 | async-start | bytes 1048576 | tf_op jit(solution)/shard_map/psum | solution.py:229
  458.0 310.7 %all-reduce.15.cloned.1.call-start = ((), (), s32[]{:S(2)}) async-start(), calls=%async_computation.14 | async-start | bytes 6291456 | tf_op jit(solution)/shard_map/psum | solution.py:248
  771.3 2.4 copy-start.4
  774.4 4.5 copy-start.10
Sparse Core Ops, SparseCore 0:
  9.6 66.1 all-gather.4
  85.9 29.0 all-gather.6
  119.9 26.3 all-reduce.6
  147.7 80.7 all-gather.8
  229.9 79.0 all-gather.10
  313.7 26.8 all-reduce.8
  349.8 28.6 all-reduce.10
  454.0 210.9 reduce-scatter.1
  667.9 29.6 all-reduce.12
  699.8 68.8 all-reduce.14
where the time goes:
time: 791 us; the launch traced here: 790 us
  waiting for transfers between devices  570 us (72%)
  blocking collectives  70.7 us (9%)
  matrix products  52.7 us (7%)
  local copies, waits for them, and re-layouts  34.8 us (4%)
  other arithmetic  33.7 us (4%)
  between operations  14.7 us (2%)
  starting transfers between devices  12.8 us (2%)
    reduce_scatter x1, waiting for transfers between devices, shards(): lax.psum_scatter(jnp.concatenate([part_qkv, part_out, part_up, part_down]...  207 us
    all_gather x1, waiting for transfers between devices, shards(): lax.all_gather(w_up, 'shard', axis=0, tiled=True)  79.5 us
    all_gather x1, waiting for transfers between devices, shards(): lax.all_gather(w_down, 'shard', axis=1, tiled=True)  74.8 us
    all_gather x1, waiting for transfers between devices, shards(): lax.all_gather(w_qkv, 'shard', axis=1, tiled=True)  66.9 us
    psum x1, blocking collectives, shards(): lax.psum((bias_qv_grad, bias_out_grad, gain_one_grad, shift_one_grad, bia...  62.3 us
    psum x1, waiting for transfers between devices, shards(): owned = lax.psum(owned.astype(jnp.bfloat16), 'ctx').astype(jnp.float32)  39.1 us
    psum x1, waiting for transfers between devices, shards(): lax.psum(back_part.astype(jnp.bfloat16), 'tp').astype(jnp.float32)  28.8 us
    psum x1, waiting for transfers between devices, shards(): lax.psum(ffn_part.astype(jnp.bfloat16), 'tp').astype(jnp.float32)  26.9 us
  transfers between devices with their start and end apart: 13, of which 11 were waited for; matrix products, arithmetic and copies ran while one was open for 5% of the time, Pallas kernels for 0%

commit v1 on v0

--- a/solution.py
+++ b/solution.py
@@ -3,9 +3,38 @@
 import jax.numpy as jnp
 from jax import lax
 from jax.sharding import PartitionSpec as P
+from jax.lax import axis_index, axis_size, ppermute
 
 HEADS = 16
 EPSILON = 1e-05
+
+
+def name_forms(in_array):
+    work_now, block_out, n_now = (axis_size("shard"), axis_index("shard"), in_array.shape[0])
+    row_list = []
+    for u, hop_no in enumerate(in_array.shape):
+        row_list.append(hop_no * work_now if u == 0 else hop_no)
+    mid_arr = lax.dynamic_update_slice_in_dim(
+        jnp.zeros(row_list, in_array.dtype), in_array, block_out * n_now, axis=0
+    )
+    v_now = odd = in_array
+    for kk in range(1, work_now // 2 + 1):
+        shelf = []
+        for u in range(work_now):
+            shelf.append((u, (u + 1) % work_now))
+        v_now = ppermute(v_now, axis_name="shard", perm=shelf)
+        mid_arr = lax.dynamic_update_slice_in_dim(
+            mid_arr, v_now, (block_out - kk) % work_now * n_now, axis=0
+        )
+        if 2 * kk < work_now:
+            kept_rows = []
+            for u in range(work_now):
+                kept_rows.append((u, (u - 1) % work_now))
+            odd = ppermute(odd, axis_name="shard", perm=kept_rows)
+            mid_arr = lax.dynamic_update_slice_in_dim(
+                mid_arr, odd, (block_out + kk) % work_now * n_now, axis=0
+            )
+    return mid_arr
 
 
 def normalize(resid, gain, shift):
@@ -70,7 +99,7 @@
     qkv_full, out_full, up_full, down_full = (
         lax.all_gather(w_qkv, "shard", axis=1, tiled=True),
         lax.all_gather(w_out, "shard", axis=1, tiled=True),
-        lax.all_gather(w_up, "shard", axis=0, tiled=True),
+        name_forms(w_up),
         lax.all_gather(w_down, "shard", axis=1, tiled=True),
     )
     local_cols = qkv_full.shape[2]

time: 791 us -> 748 us (0.946)
  waiting for transfers between devices: 570 us -> 506 us
  local copies, waits for them, and re-layouts: 34.8 us -> 50.9 us
    ppermute x0 -> x3, waiting for transfers between devices: none -> 92 us  [the longest x2 56 us: name_forms(): v_now = ppermute(v_now, axis_name='shard', perm=shelf)]
    all_gather x1 -> x0, waiting for transfers between devices: 79.5 us -> none  [shards(): lax.all_gather(w_up, 'shard', axis=0, tiled=True)]
    all_gather x1, waiting for transfers between devices: 74.8 us -> 24.6 us  [shards(): lax.all_gather(w_down, 'shard', axis=1, tiled=True)]
    psum x1, waiting for transfers between devices: 25.2 us -> 0.01 us  [shards(): lax.psum(attn_part.astype(jnp.bfloat16), 'tp').astype(jnp.float32)]
    dynamic_update_slice x0 -> x4, local copies, waits for them, and re-layouts: none -> 8.09 us  [the longest x2 4.7 us: name_forms(): lax.dynamic_update_slice_in_dim(mid_arr, v_now, (block_out - kk) % work_n...]
  transfers between devices with their start and end apart: 13 -> 15, of which waited for: 11 -> 12; matrix products, arithmetic and copies ran while one was open for 5% -> 7% of each run, Pallas kernels for 0% -> 0%
where the time goes in v1:
time: 748 us; the launch traced here: 747 us
  waiting for transfers between devices  506 us (68%)
  blocking collectives  70.7 us (9%)
  matrix products  54.2 us (7%)
  local copies, waits for them, and re-layouts  50.9 us (7%)
  other arithmetic  33.7 us (5%)
  starting transfers between devices  16.5 us (2%)
  between operations  14.4 us (2%)
    reduce_scatter x1, waiting for transfers between devices, shards(): lax.psum_scatter(jnp.concatenate([part_qkv, part_out, part_up, part_down]...  207 us
    all_gather x1, waiting for transfers between devices, shards(): lax.all_gather(w_qkv, 'shard', axis=1, tiled=True)  66.9 us
    psum x1, blocking collectives, shards(): lax.psum((bias_qv_grad, bias_out_grad, gain_one_grad, shift_one_grad, bia...  62.3 us
    ppermute x2, waiting for transfers between devices, name_forms(): v_now = ppermute(v_now, axis_name='shard', perm=shelf)  56 us
    psum x1, waiting for transfers between devices, shards(): owned = lax.psum(owned.astype(jnp.bfloat16), 'ctx').astype(jnp.float32)  39.2 us
    ppermute x1, waiting for transfers between devices, name_forms(): odd = ppermute(odd, axis_name='shard', perm=kept_rows)  36 us
    psum x1, waiting for transfers between devices, shards(): lax.psum(back_part.astype(jnp.bfloat16), 'tp').astype(jnp.float32)  28.8 us
    psum x1, waiting for transfers between devices, shards(): lax.psum(ffn_part.astype(jnp.bfloat16), 'tp').astype(jnp.float32)  26.3 us
  transfers between devices with their start and end apart: 15, of which 12 were waited for; matrix products, arithmetic and copies ran while one was open for 7% of the time, Pallas kernels for 0%

profile of v1, /device:TPU:0, one launch (start us, length us, event | category | flops | bytes accessed | tf_op | source)
XLA Modules:
  0.0 746.5 jit_solution(5344457241700051919)
XLA Ops:
  8.8 66.9 %all-gather.4.cloned.1.call-done = bf16[3,1024,512]{2,1,0:T(8,128)(2,1)} async-done(((bf16[3,256,512]{2,1,0:T(8,128)(2,1)}), bf16[3,1024,512]{2,1,0:T(8,128)(2,1)}) %all-gather.4.cloned.1.call-update) | async-done | bytes 3145744 | tf_op jit(solution)/shard_map/all_gather | solution.py:100
  75.8 3.0 add_convert_fusion
  80.0 3.5 all-to-all-start
  85.5 9.6 %all-to-all-done = bf16[1,256,3,4,128]{4,1,2,0,3:T(8,128)(2,1)S(1)} async-done(((bf16[1,256,3,4,128]{4,1,2,0,3:T(8,128)(2,1)}), bf16[1,256,3,4,128]{4,1,2,0,3:T(8,128)(2,1)S(1)}, u32[]{:S(2)}, u32[]{:S(2)}) %all-to-all-start) | async-done | bytes 786464 | tf_op jit(solution)/shard_map/all_to_all | solution.py:117
  96.7 7.9 %while.45 = (s32[]{:T(128)}, bf16[2,512,2,64]{1,3,2,0:T(8,128)(2,1)S(1)}, f32[2,2,512]{2,1,0:T(2,128)S(1)}, s32[2,512]{1,0:T(2,128)S(1)}, s32[1024]{0:T(1024)S(1...) while((s32[]{:T(128)}, ...), condition=%wide.region_3.4_spmd, body=%wide.region_0.3_spmd.sunk | while | flops 280567808 | bytes 15526005 | solution.py:137
  106.6 2.2 reduce.7
  108.9 8.4 %all_to_all.60 = bf16[4,2,16384]{2,1,0:T(2,128)(2,1)S(1)} all-to-all(bf16[4,2,16384]{2,1,0:T(2,128)(2,1)S(1)} %reshape.279), channel_id=1, replica_groups=mesh['shard'=4,'ctx'=4,'tp'=2] {'ctx'}, dimensions={0} | all-to-all | bytes 524288 | tf_op jit(solution)/shard_map/all_to_all | solution.py:141
  117.8 2.6 convolution_convert_fusion.5
  121.0 3.8 collective-permute-start.1
  124.9 24.1 %collective-permute-done = bf16[256,2048]{1,0:T(8,128)(2,1)} collective-permute-done((bf16[256,2048]{1,0:T(8,128)(2,1)S(1)}, bf16[256,2048]{1,0:T(8,128)(2,1)}, u32[]{:S(2)}, u32[]{:S(2)}) %collective-permute-start) | collective-permute-done | bytes 1048608 | tf_op jit(solution)/shard_map/ppermute | solution.py:25
  149.0 2.5 broadcast_in_dim.44
  152.5 2.3 constant_dynamic-update-slice_fusion.2
  154.9 36.0 %collective-permute-done.1 = bf16[256,2048]{1,0:T(8,128)(2,1)} collective-permute-done((bf16[256,2048]{1,0:T(8,128)(2,1)S(1)}, bf16[256,2048]{1,0:T(8,128)(2,1)}, u32[]{:S(2)}, u32[]{:S(2)}) %collective-permute-start.1) | collective-permute-done | bytes 1048608 | tf_op jit(solution)/shard_map/ppermute | solution.py:33
  190.9 2.4 constant_dynamic-update-slice_fusion.1
  193.3 31.8 %collective-permute-done.2 = bf16[256,2048]{1,0:T(8,128)(2,1)} collective-permute-done((bf16[256,2048]{1,0:T(8,128)(2,1)}, bf16[256,2048]{1,0:T(8,128)(2,1)}, u32[]{:S(2)}, u32[]{:S(2)}) %collective-permute-start.2) | collective-permute-done | bytes 1048608 | tf_op jit(solution)/shard_map/ppermute | solution.py:25
  225.1 2.3 constant_dynamic-update-slice_fusion
  230.2 5.3 multiply_convert_fusion.1
  235.5 24.6 %all-gather.8.cloned.1.call-done = bf16[2048,1024]{1,0:T(8,128)(2,1)} async-done(((bf16[2048,256]{1,0:T(8,128)(2,1)}), bf16[2048,1024]{1,0:T(8,128)(2,1)}) %all-gather.8.cloned.1.call-update) | async-done | bytes 4194320 | tf_op jit(solution)/shard_map/all_gather | solution.py:103
  260.1 4.3 convolution_convert_fusion.7
  264.4 26.3 %all-reduce.9.cloned.1.call-done = bf16[256,1024]{1,0:T(8,128)(2,1)} async-done(((bf16[256,1024]{1,0:T(8,128)(2,1)}), bf16[256,1024]{1,0:T(8,128)(2,1)}) %all-reduce.9.cloned.1.call-update) | async-done | bytes 524304 | tf_op jit(solution)/shard_map/psum | solution.py:161
  290.7 1.7 fusion.74
  294.5 2.1 fusion.76
  297.6 4.3 convolution_convert_fusion.6
  301.9 28.8 %all-reduce.11.cloned.1.call-done = bf16[256,1024]{1,0:T(8,128)(2,1)} async-done(((bf16[256,1024]{1,0:T(8,128)(2,1)}), bf16[256,1024]{1,0:T(8,128)(2,1)}) %all-reduce.11.cloned.1.call-update) | async-done | bytes 524304 | tf_op jit(solution)/shard_map/psum | solution.py:175
  330.7 1.9 multiply_reduce_fusion
  336.3 1.8 copy.118
  338.1 4.3 all-to-all-start.2
  342.4 4.6 convolution_convert_fusion.2
  349.6 12.0 %while.46 = (s32[]{:T(128)}, f32[1024,2,64]{0,2,1:T(8,128)S(1)}, f32[1024,2,64]{0,2,1:T(8,128)}, bf16[2,512,2,64]{1,3,2,0:T(8,128)(2,1)S(1)}, bf16[2,512,2,64]{1...) while((s32[]{:T(128)}, f32[1024,2,64]{0,2,1:T(8,128)S(1)}, ...), condition=%wide.region_17.18_spmd.clone, body=%wide.region_15.17_spmd.clone.sunk | while | flops 683998208 | bytes 29526284 | solution.py:227
  352.3 2.0 multiply_convert_fusion.3
  358.3 2.0 multiply_convert_fusion.3
  364.7 4.2 all-to-all-start.3
  369.0 4.5 convolution_convert_fusion.1
  375.4 8.1 %all-to-all-done.3 = bf16[1,1024,3,1,128]{4,2,3,0,1:T(4,128)(2,1)} async-done(((bf16[1,1024,3,1,128]{4,2,3,0,1:T(4,128)(2,1)}), bf16[1,1024,3,1,128]{4,2,3,0,1:T(4,128)(2,1)}, u32[]{:S(2)}, u32[]{:S(2)}) %all-to-all-start.3) | async-done | bytes 786464 | tf_op jit(solution)/shard_map/all_to_all | solution.py:242
  386.3 1.6 reshape.260
  388.0 2.7 convolution_convert_fusion.3
  390.6 4.6 copy.110
  395.3 10.9 %pad_maximum_fusion = bf16[1024,6144]{1,0:T(8,128)(2,1)} fusion(bf16[1024,2048]{1,0:T(8,128)(2,1)} %convolution_convert_fusion.1, bf16[1024,2048]{1,0:T(8,128)(2,1)} %convolution_convert_fusion.2, bf16[1024,512]{1,0:T(8,128)(2,1)} %copy.111, bf16[1024,1536]{1,0:T(8,128)(2,1)} %copy.110), kind=kLoop, calls=%fused_computation.55 | loop fusion | flops 50331648 | bytes 25165824 | tf_op jit(solution)/shard_map/concatenate | solution.py:272
  406.5 3.7 fusion.53
  410.3 207.0 %reduce-scatter.2.cloned.1.call-done = bf16[256,6144]{1,0:T(8,128)(2,1)} async-done(((bf16[1024,6144]{1,0:T(8,128)(2,1)}), bf16[256,6144]{1,0:T(8,128)(2,1)}) %reduce-scatter.2.cloned.1.call-update) | async-done | bytes 3145744 | tf_op jit(solution)/shard_map/reduce_scatter | solution.py:271
  617.6 62.3 %all-reduce = (f32[2,512]{1,0:T(2,128)}, f32[1024]{0:T(1024)}, f32[1024]{0:T(1024)}, f32[1024]{0:T(1024)}, f32[2048]{0:T(1024)}, /*index=5*/f32[1024]{0:T(1024)}, f32[1024]{0:T(1024)}, f32[1024]{0:T(1024)}) all-reduce(f32[2,512]{1,0:T(2,128)S(1)} %pad_maximum_fusion.3, ...), channel_id=1, replica_groups=mesh['shard'=4,'ctx'=4,'tp'=2] {'shard','ctx'}, use_global_device_ids=true, to_apply=%region_23.24 | all-reduce | flops 9216 | bytes 73728 | tf_op jit(solution)/shard_map/psum | solution.py:284
  679.9 2.0 fusion.61
  681.9 39.2 %all-reduce.15.cloned.1.call-done = bf16[256,6144]{1,0:T(8,128)(2,1)} async-done(((bf16[256,6144]{1,0:T(8,128)(2,1)}), bf16[256,6144]{1,0:T(8,128)(2,1)}) %all-reduce.15.cloned.1.call-update) | async-done | bytes 3145744 | tf_op jit(solution)/shard_map/psum | solution.py:277
  721.1 2.6 convert_element_type.134
  727.5 3.0 copy.112
  730.5 3.0 copy.113
  733.5 2.9 copy.115
  736.4 2.0 copy.114
  (176 shorter events, 51.8 us)
Async XLA Ops:
  7.2 68.6 %all-gather.4.cloned.1.call-start = ((), (), s32[]{:S(2)}) async-start(), calls=%async_computation.5 | async-start | bytes 3932160 | tf_op jit(solution)/shard_map/all_gather | solution.py:100
  8.8 76.0 %copy-start.15 = (s32[1,1024]{1,0:T(1,128)S(1)}, s32[1,1024]{1,0:T(1,128)}, u32[]{:S(2)}) copy-start(s32[1,1024]{1,0:T(1,128)} %param.21) | copy-start | bytes 12292
  80.0 15.1 %all-to-all-start = ((bf16[1,256,3,4,128]{4,1,2,0,3:T(8,128)(2,1)}), bf16[1,256,3,4,128]{4,1,2,0,3:T(8,128)(2,1)S(1)}, u32[]{:S(2)}, u32[]{:S(2)}) async-start(bf16[1,256,3,4,128]{4,1,2,0,3:T(8,128)(2,1)} %copy.95), calls=%async_computation | async-start | bytes 1572864 | tf_op jit(solution)/shard_map/all_to_all | solution.py:117
  83.5 34.2 %all-gather.6.cloned.1.call-start = ((), (), s32[]{:S(2)}) async-start(), calls=%async_computation.6 | async-start | bytes 1310720 | tf_op jit(solution)/shard_map/all_gather | solution.py:101
  84.3 143.2 %all-reduce.7.cloned.1.call-start = ((), (), s32[]{:S(2)}) async-start(), calls=%async_computation.7 | async-start | bytes 1048576 | tf_op jit(solution)/shard_map/psum | solution.py:151
  104.6 0.7 copy-start.17
  105.7 15.3 %copy-start.11 = (bf16[256,2048]{1,0:T(8,128)(2,1)S(1)}, bf16[256,2048]{1,0:T(8,128)(2,1)}, u32[]{:S(2)}) copy-start(bf16[256,2048]{1,0:T(8,128)(2,1)} %param.28) | copy-start | bytes 3145732
  117.7 31.3 %copy-start.8 = (bf16[1,256,4,1,128]{1,4,2,3,0:T(8,128)(2,1)}, bf16[1,256,4,1,128]{1,4,2,3,0:T(8,128)(2,1)S(1)}, u32[]{:S(2)}) copy-start(bf16[1,256,4,1,128]{1,4,2,3,0:T(8,128)(2,1)S(1)} %copy.100) | copy-start | bytes 786436
  120.3 139.7 %all-gather.8.cloned.1.call-start = ((), (), s32[]{:S(2)}) async-start(), calls=%async_computation.8 | async-start | bytes 5242880 | tf_op jit(solution)/shard_map/all_gather | solution.py:103
  120.9 169.8 %all-reduce.9.cloned.1.call-start = ((), (), s32[]{:S(2)}) async-start(), calls=%async_computation.9 | async-start | bytes 1048576 | tf_op jit(solution)/shard_map/psum | solution.py:161
  121.0 28.0 %collective-permute-start = (bf16[256,2048]{1,0:T(8,128)(2,1)S(1)}, bf16[256,2048]{1,0:T(8,128)(2,1)}, u32[]{:S(2)}, u32[]{:S(2)}) collective-permute-start(bf16[256,2048]{1,0:T(8,128)(2,1)S(1)} %copy-done.11), channel_id=1, source_target_pairs={{0,8},{8,16},{16,24},{24,0},{1,9},{9,17},{17,25},{25,1},{2,10},{10... | collective-permute-start | bytes 3145736 | tf_op jit(solution)/shard_map/ppermute | solution.py:25
  121.0 69.9 %collective-permute-start.1 = (bf16[256,2048]{1,0:T(8,128)(2,1)S(1)}, bf16[256,2048]{1,0:T(8,128)(2,1)}, u32[]{:S(2)}, u32[]{:S(2)}) collective-permute-start(bf16[256,2048]{1,0:T(8,128)(2,1)S(1)} %copy-done.11), channel_id=1, source_target_pairs={{0,24},{8,0},{16,8},{24,16},{1,25},{9,1},{17,9},{25,17},{2,26},{10... | collective-permute-start | bytes 3145736 | tf_op jit(solution)/shard_map/ppermute | solution.py:33
  149.0 76.1 %collective-permute-start.2 = (bf16[256,2048]{1,0:T(8,128)(2,1)}, bf16[256,2048]{1,0:T(8,128)(2,1)}, u32[]{:S(2)}, u32[]{:S(2)}) collective-permute-start(bf16[256,2048]{1,0:T(8,128)(2,1)} %collective-permute-done), channel_id=1, source_target_pairs={{0,8},{8,16},{16,24},{24,0},{1,9},{9,17},{17,25},{25,1},{2,10},{10... | collective-permute-start | bytes 3145736 | tf_op jit(solution)/shard_map/ppermute | solution.py:25
  151.5 76.0 %copy-start = (bf16[1,256,1024]{2,1,0:T(8,128)(2,1)S(1)}, bf16[1,256,1024]{2,1,0:T(8,128)(2,1)}, u32[]{:S(2)}) copy-start(bf16[1,256,1024]{2,1,0:T(8,128)(2,1)} %param.19) | copy-start | bytes 1572868
  151.5 76.0 %copy-start.16 = (f32[1024]{0:T(1024)S(1)}, f32[1024]{0:T(1024)}, u32[]{:S(2)}) copy-start(f32[1024]{0:T(1024)} %param.25) | copy-start | bytes 12292
  152.5 77.6 %copy-start.19 = (f32[1024]{0:T(1024)S(1)}, f32[1024]{0:T(1024)}, u32[]{:S(2)}) copy-start(f32[1024]{0:T(1024)} %param.26) | copy-start | bytes 12292
  152.5 77.6 %copy-start.20 = (f32[1024]{0:T(1024)S(1)}, f32[1024]{0:T(1024)}, u32[]{:S(2)}) copy-start(f32[1024]{0:T(1024)} %param.27) | copy-start | bytes 12292
  152.5 77.6 %copy-start.25 = (f32[2048]{0:T(1024)S(1)}, f32[2048]{0:T(1024)}, u32[]{:S(2)}) copy-start(f32[2048]{0:T(1024)} %param.29) | copy-start | bytes 24580
  235.5 57.0 %copy-start.10 = (bf16[256,2048]{1,0:T(8,128)(2,1)}, bf16[256,2048]{1,0:T(8,128)(2,1)S(1)}, u32[]{:S(2)}) copy-start(bf16[256,2048]{1,0:T(8,128)(2,1)S(1)} %get-tuple-element.422) | copy-start | bytes 3145732
  235.5 55.2 %copy-start.1 = (bf16[256,1024]{1,0:T(8,128)(2,1)S(1)}, bf16[256,1024]{1,0:T(8,128)(2,1)}, u32[]{:S(2)}) copy-start(bf16[256,1024]{1,0:T(8,128)(2,1)} %all-reduce.7.cloned.1.call-done) | copy-start | bytes 1572868
  235.5 55.2 %copy-start.22 = (f32[1024]{0:T(1024)S(1)}, f32[1024]{0:T(1024)}, u32[]{:S(2)}) copy-start(f32[1024]{0:T(1024)} %param.31) | copy-start | bytes 12292
  260.0 32.7 %copy-start.5 = (bf16[1,256,1024]{2,1,0:T(8,128)(2,1)S(1)}, bf16[1,256,1024]{2,1,0:T(8,128)(2,1)}, u32[]{:S(2)}) copy-start(bf16[1,256,1024]{2,1,0:T(8,128)(2,1)} %param.20) | copy-start | bytes 1572868
  260.1 32.7 %copy-start.21 = (f32[1024]{0:T(1024)S(1)}, f32[1024]{0:T(1024)}, u32[]{:S(2)}) copy-start(f32[1024]{0:T(1024)} %param.32) | copy-start | bytes 12292
  264.3 28.9 %copy-start.23 = (f32[1024]{0:T(1024)S(1)}, f32[1024]{0:T(1024)}, u32[]{:S(2)}) copy-start(f32[1024]{0:T(1024)} %param.33) | copy-start | bytes 12292
  264.4 66.4 %all-reduce.11.cloned.1.call-start = ((), (), s32[]{:S(2)}) async-start(), calls=%async_computation.10 | async-start | bytes 1048576 | tf_op jit(solution)/shard_map/psum | solution.py:175
  290.7 3.8 copy-start.24
  290.7 3.8 copy-start.26
  296.6 1.0 copy-start.12
  330.7 4.4 copy-start.7
  334.2 1.0 copy-start.2
  338.1 10.1 %all-to-all-start.2 = ((bf16[1,256,4,128]{1,3,0,2:T(8,128)(2,1)}), bf16[1,256,4,128]{1,3,0,2:T(8,128)(2,1)}, u32[]{:S(2)}, u32[]{:S(2)}) async-start(bf16[1,256,4,128]{1,3,0,2:T(8,128)(2,1)} %bitcast.233), calls=%async_computation.2 | async-start | bytes 524288 | tf_op jit(solution)/shard_map/all_to_all | solution.py:184
  349.7 1.2 copy-start.13
  350.9 1.4 copy-start.18
  352.3 2.0 copy-start.14
  355.7 1.2 copy-start.13
  356.9 1.4 copy-start.18
  358.3 2.0 copy-start.14
  364.7 18.7 %all-to-all-start.3 = ((bf16[1,1024,3,1,128]{4,2,3,0,1:T(4,128)(2,1)}), bf16[1,1024,3,1,128]{4,2,3,0,1:T(4,128)(2,1)}, u32[]{:S(2)}, u32[]{:S(2)}) async-start(bf16[1,1024,3,1,128]{4,2,3,0,1:T(4,128)(2,1)} %copy.106), calls=%async_computation.3 | async-start | bytes 2097152 | tf_op jit(solution)/shard_map/all_to_all | solution.py:242
  369.0 4.6 copy-start.3
  369.0 4.6 copy-start.9
  369.0 248.3 %reduce-scatter.2.cloned.1.call-start = ((), (), s32[]{:S(2)}) async-start(), calls=%async_computation.12 | async-start | bytes 15728640 | tf_op jit(solution)/shard_map/reduce_scatter | solution.py:271
  406.2 211.2 %copy-start.6 = (bf16[1,256,1024]{2,1,0:T(8,128)(2,1)S(1)}, bf16[1,256,1024]{2,1,0:T(8,128)(2,1)}, u32[]{:S(2)}) copy-start(bf16[1,256,1024]{2,1,0:T(8,128)(2,1)} %param.20) | copy-start | bytes 1572868
  406.2 273.7 %all-reduce.13.cloned.1.call-start = ((), (), s32[]{:S(2)}) async-start(), calls=%async_computation.11 | async-start | bytes 1048576 | tf_op jit(solution)/shard_map/psum | solution.py:258
  410.2 310.9 %all-reduce.15.cloned.1.call-start = ((), (), s32[]{:S(2)}) async-start(), calls=%async_computation.13 | async-start | bytes 6291456 | tf_op jit(solution)/shard_map/psum | solution.py:277
  723.7 2.4 copy-start.4
Sparse Core Ops, SparseCore 0:
  9.6 66.1 all-gather.3
  85.9 29.0 all-gather.5
  120.5 26.3 all-reduce.6
  148.3 111.7 all-gather.7
  264.5 26.1 all-reduce.8
  302.0 28.6 all-reduce.10
  406.3 210.9 reduce-scatter.1
  620.2 29.6 all-reduce.12
  652.3 68.7 all-reduce.14
